TPU v7x, 32 devices: a whole 2x2x4 slice. The times are simulated.
32 devices in a mesh: dp: 8 (over z, y), tensor: 4 (over x, core).
Axes of the slice: x: 2, y: 2, z: 4, core: 2. Of those that a mesh axis runs over, the one named last changes fastest.
Arguments:
- tokens: bfloat16 [8192, 768], P('dp'), may hold values from -6 to 6
- cotangent: bfloat16 [8192, 768], P('dp'), may hold values from -6 to 6
- item_count: int32 [8], P('dp'), may hold values from 0 to 1, as said below
- timestep: int32 [8], P('dp'), may hold values from 0 to 999
- class_id: int32 [8], P('dp'), may hold values from 0 to 1000
- class_table: bfloat16 [1001, 768], replicated, may hold values from -6 to 6
- w_mod: bfloat16 [4608, 768], replicated, may hold values from -0.21875 to 0.21875
- b_mod: bfloat16 [4608], replicated, may hold values from -3 to 3
- k_att: bfloat16 [9, 768], replicated, may hold values from -2 to 2
- w_qkv: bfloat16 [768, 3, 768], P(None, None, 'tensor'), may hold values from -0.21875 to 0.21875
- w_out: bfloat16 [768, 768], P(None, 'tensor'), may hold values from -0.875 to 0.875
- b_out: bfloat16 [768], replicated, may hold values from -2 to 2
- w_up: bfloat16 [768, 3072], P(None, 'tensor'), may hold values from -0.21875 to 0.21875
- b_up: bfloat16 [3072], P('tensor'), may hold values from -2 to 2
- k_ffn: bfloat16 [9, 3072], P(None, 'tensor'), may hold values from -2 to 2
- w_down: bfloat16 [768, 3072], P(None, 'tensor'), may hold values from -0.109375 to 0.109375
- b_down: bfloat16 [768], replicated, may hold values from -2 to 2
Outputs:
- block_out: bfloat16 [8192, 768], P(('dp', 'tensor'))
- grad_tokens: float32 [8192, 768], P(('dp', 'tensor'))
- grad_class_table: float32 [1001, 768], replicated
- grad_w_mod: float32 [4608, 768], P('dp')
- grad_b_mod: float32 [4608], replicated
- grad_k_att: float32 [9, 768], replicated
- grad_w_qkv: float32 [768, 3, 768], P('dp', None, 'tensor')
- grad_w_out: float32 [768, 768], P('dp', 'tensor')
- grad_b_out: float32 [768], replicated
- grad_w_up: float32 [768, 3072], P('dp', 'tensor')
- grad_b_up: float32 [3072], P('tensor')
- grad_k_ffn: float32 [9, 3072], P(None, 'tensor')
- grad_w_down: float32 [768, 3072], P('dp', 'tensor')
- grad_b_down: float32 [768], replicated
Inputs may be any that keep to these rules, and one draw needn't show every extreme that they name: Item slots below item_count of their dp index hold live items, the others padding; some index of dp has all 1 slots live and some none.
All inputs are finite; a program needn't handle non-finite values.
Results may differ from a plain program's by a relative error of at most 0.028.
The roundings to bfloat16 on the way count: a program that leaves them out, or rounds other values in their place, can miss the bound.
Values may be sent and summed in bfloat16 or wider, within the bound.
No kernel may reach another device: no remote copies, remote signals or barrier semaphores. Data moves between devices by JAX's collectives and lax.ppermute only.
A program may use at most 192 MiB of HBM per device.

v0:
```python
import math
import jax
import jax.numpy as jnp
from jax import lax
from jax.sharding import PartitionSpec as P

HEAD_DIM = 64
SIDE = 32
norm_eps = 1e-06
score_scale = 0.125
highest = lax.Precision.HIGHEST


def layer_norm(values):
    center = values - jnp.mean(values, axis=-1, keepdims=True)
    return center * lax.rsqrt(jnp.mean(center * center, axis=-1, keepdims=True) + norm_eps)


def time_features(timestep, width):
    half_width = width // 2
    freqs = jnp.exp(-math.log(10000.0) * jnp.arange(half_width, dtype=jnp.float32) / half_width)
    angles = timestep.astype(jnp.float32)[:, None] * freqs[None, :]
    return jnp.concatenate([jnp.cos(angles), jnp.sin(angles)], axis=1)


def depthwise(field, kernel):
    grid_side = field.shape[1]
    padded = jnp.pad(field, ((0, 0), (1, 1), (1, 1), (0, 0)))
    total = jnp.zeros_like(field)
    for vertical in range(3):
        for horizontal in range(3):
            total = (
                total
                + kernel[vertical * 3 + horizontal]
                * padded[:, vertical : vertical + grid_side, horizontal : horizontal + grid_side]
            )
    return total


def depthwise_back(field, grad_field, kernel):
    grid_side = field.shape[1]
    padded_in = jnp.pad(field, ((0, 0), (1, 1), (1, 1), (0, 0)))
    padded_grad = jnp.pad(grad_field, ((0, 0), (1, 1), (1, 1), (0, 0)))
    input_grad = jnp.zeros_like(field)
    kernel_rows = []
    for vertical in range(3):
        for horizontal in range(3):
            input_grad = (
                input_grad
                + kernel[vertical * 3 + horizontal]
                * padded_grad[
                    :,
                    2 - vertical : 2 - vertical + grid_side,
                    2 - horizontal : 2 - horizontal + grid_side,
                ]
            )
            kernel_rows.append(
                jnp.sum(
                    grad_field
                    * padded_in[
                        :, vertical : vertical + grid_side, horizontal : horizontal + grid_side
                    ],
                    axis=(0, 1, 2),
                )
            )
    return (input_grad, jnp.stack(kernel_rows))


def to_groups(values, items_here):
    half_side = SIDE // 2
    trailing = values.shape[1:]
    shaped = values.reshape((items_here, half_side, 2, half_side, 2) + trailing)
    axes_order = (0, 2, 4, 1, 3) + tuple(range(5, 5 + len(trailing)))
    return shaped.transpose(axes_order).reshape((items_here * 4, half_side * half_side) + trailing)


def from_groups(values, items_here):
    half_side = SIDE // 2
    trailing = values.shape[2:]
    shaped = values.reshape((items_here, 2, 2, half_side, half_side) + trailing)
    axes_order = (0, 3, 1, 4, 2) + tuple(range(5, 5 + len(trailing)))
    return shaped.transpose(axes_order).reshape((items_here * SIDE * SIDE,) + trailing)


def split_project(project, items_here):
    grouped = to_groups(project.reshape(project.shape[0], 3, -1, HEAD_DIM), items_here)
    return (grouped[:, :, 0], grouped[:, :, 1], grouped[:, :, 2])


def attend(project, items_here):
    query, keys, vals = split_project(project, items_here)
    scores = (
        jnp.einsum("bqhd,bkhd->bhqk", query, keys, preferred_element_type=jnp.float32) * score_scale
    )
    top_score = jnp.max(scores, axis=-1, keepdims=True)
    log_total = top_score + jnp.log(jnp.sum(jnp.exp(scores - top_score), axis=-1, keepdims=True))
    probs_low = jnp.exp(scores - log_total).astype(jnp.bfloat16)
    attended = jnp.einsum("bhqk,bkhd->bqhd", probs_low, vals, preferred_element_type=jnp.float32)
    merged = from_groups(attended, items_here)
    return (merged.reshape(merged.shape[0], -1).astype(jnp.bfloat16), log_total)


def attend_back(project, log_total, grad_attended, items_here):
    query, keys, vals = split_project(project, items_here)
    grad_grouped = to_groups(
        grad_attended.reshape(grad_attended.shape[0], -1, HEAD_DIM), items_here
    )
    scores = (
        jnp.einsum("bqhd,bkhd->bhqk", query, keys, preferred_element_type=jnp.float32) * score_scale
    )
    probs = jnp.exp(scores - log_total)
    probs_low = probs.astype(jnp.bfloat16)
    grad_probs = jnp.einsum(
        "bqhd,bkhd->bhqk", grad_grouped, vals, preferred_element_type=jnp.float32
    )
    grad_scores = (
        probs * (grad_probs - jnp.sum(probs * grad_probs, axis=-1, keepdims=True))
    ).astype(jnp.bfloat16)
    grad_query = (
        jnp.einsum("bhqk,bkhd->bqhd", grad_scores, keys, preferred_element_type=jnp.float32)
        * score_scale
    )
    grad_keys = (
        jnp.einsum("bhqk,bqhd->bkhd", grad_scores, query, preferred_element_type=jnp.float32)
        * score_scale
    )
    grad_vals = jnp.einsum(
        "bhqk,bqhd->bkhd", probs_low, grad_grouped, preferred_element_type=jnp.float32
    )
    stacked = jnp.stack([grad_query, grad_keys, grad_vals], axis=2).astype(jnp.bfloat16)
    merged = from_groups(stacked, items_here)
    return merged.reshape(merged.shape[0], 3, -1)


def contract_last(left, right):
    return lax.dot_general(
        left, right, (((1,), (1,)), ((), ())), preferred_element_type=jnp.float32
    )


def contract_first(left, right):
    return lax.dot_general(
        left, right, (((0,), (0,)), ((), ())), preferred_element_type=jnp.float32
    )


def spread_rows(row_hot, table):
    return jnp.dot(row_hot, table, precision=highest, preferred_element_type=jnp.float32)


def item_sums(row_hot, values):
    return lax.dot_general(
        row_hot,
        values,
        (((0,), (0,)), ((), ())),
        precision=highest,
        preferred_element_type=jnp.float32,
    )


def shards(
    tokens,
    cotangent,
    item_count,
    timestep,
    class_id,
    class_table,
    w_mod,
    b_mod,
    k_att,
    w_qkv,
    w_out,
    b_out,
    w_up,
    b_up,
    k_ffn,
    w_down,
    b_down,
):
    items_here = timestep.shape[0]
    total_rows = tokens.shape[0]
    width = tokens.shape[1]
    item_rows = total_rows // items_here
    share_rows = total_rows // lax.axis_size("tensor")
    share_start = lax.axis_index("tensor") * share_rows
    live = (jnp.arange(items_here) < item_count[0]).astype(jnp.float32)
    row_item = (share_start + jnp.arange(share_rows)) // item_rows
    row_hot = (row_item[:, None] == jnp.arange(items_here)[None, :]).astype(jnp.float32)
    live_rows = spread_rows(row_hot, live[:, None])
    k_att_f = k_att.astype(jnp.float32)
    k_ffn_f = k_ffn.astype(jnp.float32)
    one_hot = class_id[:, None] == jnp.arange(class_table.shape[0])[None, :]
    cond = time_features(timestep, width) + jnp.dot(
        one_hot.astype(jnp.bfloat16), class_table, preferred_element_type=jnp.float32
    )
    act_low = jax.nn.silu(cond).astype(jnp.bfloat16)
    modulate = contract_last(act_low, w_mod) + b_mod.astype(jnp.float32)
    pieces = jnp.split(modulate, 6, axis=1)
    shift_att = pieces[0][:, None, :]
    scale_att = pieces[1][:, None, :]
    scale_att_rows = spread_rows(row_hot, pieces[1])
    gate_att_rows = spread_rows(row_hot, pieces[2])
    shift_ffn_rows = spread_rows(row_hot, pieces[3])
    scale_ffn_rows = spread_rows(row_hot, pieces[4])
    gate_ffn_rows = spread_rows(row_hot, pieces[5])
    x_flat = tokens.astype(jnp.float32)
    x_items = x_flat.reshape(items_here, item_rows, width)

    def forward_pass(source):
        normed = layer_norm(source)
        shaped = normed * (1.0 + scale_att) + shift_att
        mixed = (
            depthwise(shaped.reshape(items_here, SIDE, SIDE, width), k_att_f)
            .reshape(total_rows, width)
            .astype(jnp.bfloat16)
        )
        project = jnp.einsum(
            "td,dcj->tcj", mixed, w_qkv, preferred_element_type=jnp.float32
        ).astype(jnp.bfloat16)
        attended, log_total = attend(project, items_here)
        branch = lax.psum_scatter(
            contract_last(attended, w_out).astype(jnp.bfloat16),
            "tensor",
            scatter_dimension=0,
            tiled=True,
        ).astype(jnp.float32) + b_out.astype(jnp.float32)
        source_share = lax.dynamic_slice_in_dim(
            source.reshape(total_rows, width), share_start, share_rows, 0
        )
        middle = source_share + gate_att_rows * branch
        normed_ffn = layer_norm(middle)
        shaped_share = (normed_ffn * (1.0 + scale_ffn_rows) + shift_ffn_rows).astype(jnp.bfloat16)
        shaped_ffn = lax.all_gather(shaped_share, "tensor", axis=0, tiled=True)
        hidden = jnp.dot(shaped_ffn, w_up, preferred_element_type=jnp.float32) + b_up.astype(
            jnp.float32
        )
        convolved = depthwise(hidden.reshape(items_here, SIDE, SIDE, -1), k_ffn_f).reshape(
            total_rows, -1
        )
        activated = jax.nn.gelu(convolved).astype(jnp.bfloat16)
        branch_ffn = lax.psum_scatter(
            contract_last(activated, w_down).astype(jnp.bfloat16),
            "tensor",
            scatter_dimension=0,
            tiled=True,
        ).astype(jnp.float32) + b_down.astype(jnp.float32)
        result = middle + gate_ffn_rows * branch_ffn
        return (
            normed,
            shaped,
            mixed,
            project,
            attended,
            log_total,
            branch,
            middle,
            normed_ffn,
            shaped_ffn,
            hidden,
            convolved,
            activated,
            branch_ffn,
            result,
        )

    saved = forward_pass(x_items)
    block_out = (saved[14] * live_rows).astype(jnp.bfloat16)
    again = lax.optimization_barrier((x_items, block_out))[0]
    saved = forward_pass(again)
    (
        normed,
        shaped,
        mixed,
        project,
        attended,
        log_total,
        branch,
        middle,
        normed_ffn,
        shaped_ffn,
        hidden,
        convolved,
        activated,
        branch_ffn,
        result,
    ) = saved
    cot_share = lax.dynamic_slice_in_dim(cotangent, share_start, share_rows, 0)
    grad_out = cot_share.astype(jnp.float32) * live_rows
    grad_gate_ffn = item_sums(row_hot, grad_out * branch_ffn)
    grad_branch_share = (grad_out * gate_ffn_rows).astype(jnp.bfloat16)
    grad_branch_ffn = lax.all_gather(grad_branch_share, "tensor", axis=0, tiled=True)
    grad_b_down = jnp.sum(grad_branch_ffn.astype(jnp.float32), axis=0)
    grad_w_down = contract_first(grad_branch_ffn, activated)
    grad_activated = jnp.dot(grad_branch_ffn, w_down, preferred_element_type=jnp.float32)
    gelu_value, gelu_back = jax.vjp(jax.nn.gelu, convolved)
    grad_convolved = gelu_back(grad_activated)[0]
    grad_hidden, grad_k_ffn = depthwise_back(
        hidden.reshape(items_here, SIDE, SIDE, -1),
        grad_convolved.reshape(items_here, SIDE, SIDE, -1),
        k_ffn_f,
    )
    grad_hidden = grad_hidden.reshape(total_rows, -1).astype(jnp.bfloat16)
    grad_b_up = jnp.sum(grad_hidden.astype(jnp.float32), axis=0)
    grad_w_up = contract_first(shaped_ffn, grad_hidden)
    grad_shaped_ffn = lax.psum_scatter(
        contract_last(grad_hidden, w_up).astype(jnp.bfloat16),
        "tensor",
        scatter_dimension=0,
        tiled=True,
    ).astype(jnp.float32)
    grad_scale_ffn = item_sums(row_hot, grad_shaped_ffn * normed_ffn)
    grad_shift_ffn = item_sums(row_hot, grad_shaped_ffn)
    norm_value, norm_back_ffn = jax.vjp(layer_norm, middle)
    grad_middle = grad_out + norm_back_ffn(grad_shaped_ffn * (1.0 + scale_ffn_rows))[0]
    grad_gate_att = item_sums(row_hot, grad_middle * branch)
    grad_attn_share = (grad_middle * gate_att_rows).astype(jnp.bfloat16)
    grad_branch = lax.all_gather(grad_attn_share, "tensor", axis=0, tiled=True)
    grad_b_out = jnp.sum(grad_branch.astype(jnp.float32), axis=0)
    grad_w_out = contract_first(grad_branch, attended)
    grad_attended = jnp.dot(grad_branch, w_out, preferred_element_type=jnp.float32).astype(
        jnp.bfloat16
    )
    grad_project = attend_back(project, log_total, grad_attended, items_here)
    grad_w_qkv = jnp.einsum("td,tcj->dcj", mixed, grad_project, preferred_element_type=jnp.float32)
    grad_mixed_share = lax.psum_scatter(
        jnp.einsum("tcj,dcj->td", grad_project, w_qkv, preferred_element_type=jnp.float32).astype(
            jnp.bfloat16
        ),
        "tensor",
        scatter_dimension=0,
        tiled=True,
    )
    grad_mixed = lax.all_gather(grad_mixed_share, "tensor", axis=0, tiled=True).astype(jnp.float32)
    grad_shaped, grad_k_att = depthwise_back(
        shaped.reshape(items_here, SIDE, SIDE, width),
        grad_mixed.reshape(items_here, SIDE, SIDE, width),
        k_att_f,
    )
    grad_shaped_share = lax.dynamic_slice_in_dim(
        grad_shaped.reshape(total_rows, width), share_start, share_rows, 0
    )
    normed_share = lax.dynamic_slice_in_dim(
        normed.reshape(total_rows, width), share_start, share_rows, 0
    )
    grad_scale_att = item_sums(row_hot, grad_shaped_share * normed_share)
    grad_shift_att = item_sums(row_hot, grad_shaped_share)
    x_share = lax.dynamic_slice_in_dim(x_flat, share_start, share_rows, 0)
    norm_first, norm_back_att = jax.vjp(layer_norm, x_share)
    grad_tokens = grad_middle + norm_back_att(grad_shaped_share * (1.0 + scale_att_rows))[0]
    mod_partial = jnp.concatenate(
        [
            grad_shift_att,
            grad_scale_att,
            grad_gate_att,
            grad_shift_ffn,
            grad_scale_ffn,
            grad_gate_ffn,
        ],
        axis=1,
    )
    grad_modulate = lax.psum(mod_partial, "tensor").astype(jnp.bfloat16)
    grad_b_mod = jnp.sum(grad_modulate.astype(jnp.float32), axis=0)
    grad_w_mod = contract_first(grad_modulate, act_low)
    grad_act = jnp.dot(grad_modulate, w_mod, preferred_element_type=jnp.float32)
    silu_value, silu_back = jax.vjp(jax.nn.silu, cond)
    grad_cond = silu_back(grad_act)[0]
    grad_class = lax.dot_general(
        one_hot.astype(jnp.float32),
        grad_cond,
        (((0,), (0,)), ((), ())),
        precision=highest,
        preferred_element_type=jnp.float32,
    )
    summed_qkv, summed_out, summed_up, summed_down, summed_mod = (
        lax.psum_scatter(grad_w_qkv, "dp", scatter_dimension=0, tiled=True),
        lax.psum_scatter(grad_w_out, "dp", scatter_dimension=0, tiled=True),
        lax.psum_scatter(grad_w_up, "dp", scatter_dimension=0, tiled=True),
        lax.psum_scatter(grad_w_down, "dp", scatter_dimension=0, tiled=True),
        lax.psum_scatter(grad_w_mod, "dp", scatter_dimension=0, tiled=True),
    )
    small_sums = lax.psum(
        (grad_k_att, grad_k_ffn, grad_b_up, grad_b_out, grad_b_down, grad_b_mod, grad_class), "dp"
    )
    (
        summed_k_att,
        summed_k_ffn,
        summed_b_up,
        summed_b_out,
        summed_b_down,
        summed_b_mod,
        summed_class,
    ) = small_sums
    return (
        block_out,
        grad_tokens,
        summed_class,
        summed_mod,
        summed_b_mod,
        summed_k_att,
        summed_qkv,
        summed_out,
        summed_b_out,
        summed_up,
        summed_b_up,
        summed_k_ffn,
        summed_down,
        summed_b_down,
    )


def solution(mesh):
    placed = (
        P("dp", None),
        P("dp", None),
        P("dp"),
        P("dp"),
        P("dp"),
        P(),
        P(),
        P(),
        P(),
        P(None, None, "tensor"),
        P(None, "tensor"),
        P(),
        P(None, "tensor"),
        P("tensor"),
        P(None, "tensor"),
        P(None, "tensor"),
        P(),
    )
    return jax.shard_map(
        shards,
        mesh=mesh,
        in_specs=placed,
        out_specs=(
            P(("dp", "tensor"), None),
            P(("dp", "tensor"), None),
            P(),
            P("dp", None),
            P(),
            P(),
            P("dp", None, "tensor"),
            P("dp", "tensor"),
            P(),
            P("dp", "tensor"),
            P("tensor"),
            P(None, "tensor"),
            P("dp", "tensor"),
            P(),
        ),
        check_vma=False,
    )
```

profile of v0, /device:TPU:0, one launch (start us, length us, event | category | flops | bytes accessed | tf_op | source)
XLA Modules:
  0.0 1077.7 jit_solution(4446822066755356792)
XLA Ops:
  13.5 5.1 convolution_reduce_fusion
  20.1 4.5 fusion.23
  27.6 5.4 reshape_reshape.15
  42.9 27.1 %reduce-scatter.12.cloned.1.call-done = bf16[256,768]{1,0:T(8,128)(2,1)} async-done(((bf16[1024,768]{1,0:T(8,128)(2,1)}), bf16[256,768]{1,0:T(8,128)(2,1)}) %reduce-scatter.12.cloned.1.call-update) | async-done | bytes 393232 | tf_op jit(solution)/shard_map/reduce_scatter | solution.py:221
  76.5 19.5 %all-gather.6.cloned.1.call-done = bf16[1024,768]{1,0:T(8,128)(2,1)} async-done(((bf16[256,768]{1,0:T(8,128)(2,1)}), bf16[1024,768]{1,0:T(8,128)(2,1)}) %all-gather.6.cloned.1.call-update) | async-done | bytes 1572880 | tf_op jit(solution)/shard_map/all_gather | solution.py:233
  99.3 4.4 fusion.39
  110.6 25.3 %reduce-scatter.14.cloned.1.call-done = bf16[256,768]{1,0:T(8,128)(2,1)} async-done(((bf16[1024,768]{1,0:T(8,128)(2,1)}), bf16[256,768]{1,0:T(8,128)(2,1)}) %reduce-scatter.14.cloned.1.call-update) | async-done | bytes 393232 | tf_op jit(solution)/shard_map/reduce_scatter | solution.py:241
  141.8 4.5 add_convert_fusion
  149.2 5.4 reshape_reshape.16
  167.4 28.3 %reduce-scatter.16.cloned.1.call-done = bf16[256,768]{1,0:T(8,128)(2,1)} async-done(((bf16[1024,768]{1,0:T(8,128)(2,1)}), bf16[256,768]{1,0:T(8,128)(2,1)}) %reduce-scatter.16.cloned.1.call-update) | async-done | bytes 393232 | tf_op jit(solution)/shard_map/reduce_scatter | solution.py:221
  200.1 18.9 %all-gather.10.cloned.1.call-done = bf16[1024,768]{1,0:T(8,128)(2,1)} async-done(((bf16[256,768]{1,0:T(8,128)(2,1)}), bf16[1024,768]{1,0:T(8,128)(2,1)}) %all-gather.10.cloned.1.call-update) | async-done | bytes 1572880 | tf_op jit(solution)/shard_map/all_gather | solution.py:233
  223.9 5.7 multiply_add_fusion
  229.6 10.6 all-gather.8.cloned.1.call-done
  240.2 8.5 multiply_reduce_fusion.4
  250.4 5.1 convert_reduce_fusion.1
  259.3 28.3 %reduce-scatter.18.cloned.1.call-done = bf16[256,768]{1,0:T(8,128)(2,1)} async-done(((bf16[1024,768]{1,0:T(8,128)(2,1)}), bf16[256,768]{1,0:T(8,128)(2,1)}) %reduce-scatter.18.cloned.1.call-update) | async-done | bytes 393232 | tf_op jit(solution)/shard_map/reduce_scatter | solution.py:305
  294.1 19.6 %all-gather.12.cloned.1.call-done = bf16[1024,768]{1,0:T(8,128)(2,1)} async-done(((bf16[256,768]{1,0:T(8,128)(2,1)}), bf16[1024,768]{1,0:T(8,128)(2,1)}) %all-gather.12.cloned.1.call-update) | async-done | bytes 1572880 | tf_op jit(solution)/shard_map/all_gather | solution.py:317
  335.0 4.4 bitcast_convert_fusion
  339.5 28.3 %reduce-scatter.20.cloned.1.call-done = bf16[256,768]{1,0:T(8,128)(2,1)} async-done(((bf16[1024,768]{1,0:T(8,128)(2,1)}), bf16[256,768]{1,0:T(8,128)(2,1)}) %reduce-scatter.20.cloned.1.call-update) | async-done | bytes 393232 | tf_op jit(solution)/shard_map/reduce_scatter | solution.py:325
  370.9 4.7 fusion.154
  383.2 4.7 fusion.152
  390.9 4.4 fusion.72
  400.9 18.9 %reduce-scatter.22.cloned.1.call-done = bf16[256,768]{1,0:T(8,128)(2,1)} async-done(((bf16[1024,768]{1,0:T(8,128)(2,1)}), bf16[256,768]{1,0:T(8,128)(2,1)}) %reduce-scatter.22.cloned.1.call-update) | async-done | bytes 393232 | tf_op jit(solution)/shard_map/reduce_scatter | solution.py:241
  421.5 11.8 %psum.56 = bf16[1,4608]{1,0:T(2,128)(2,1)S(1)} all-reduce(f32[1,4608]{1,0:T(1,128)S(1)} %convolution_dynamic-update-slice_fusion.1), channel_id=1, replica_groups=mesh['dp'=8,'tensor'=4] {'tensor'}, use_global_device_ids=true, to_apply=%region_25.26 | all-reduce | flops 4608 | bytes 27648 | tf_op jit(solution)/shard_map/psum | solution.py:361
  439.7 6.0 broadcast_multiply_fusion
  446.7 13.3 %multiply_reduce_fusion = (f32[768]{0:T(1024)S(1)}, f32[768]{0:T(1024)S(1)}, f32[768]{0:T(1024)S(1)}, f32[768]{0:T(1024)S(1)}, f32[768]{0:T(1024)S(1)}, /*index=...) fusion(f32[1,32,32,768]{3,2,1,0:T(8,128)} %bitcast.206, f32[1024,768]{1,0:T(8,128)} %copy-done.11), kind=kLoop, calls=%fused_computation.141 | loop fusion | flops 12576768 | bytes 6316032 | tf_op jit(solution)/shard_map/reduce_sum | solution.py:58
  468.2 40.3 %all-reduce.11 = (f32[4608]{0:T(1024)}, f32[9,768]{1,0:T(8,128)}, f32[768]{0:T(1024)}, f32[768]{0:T(1024)}, f32[9,768]{1,0:T(8,128)}, /*index=5*/f32[768]{0:T(1024)}) all-reduce(bf16[4608]{0:T(1024)(128)(2,1)S(1)} %convert_reduce_fusion.4, f32[9,768]{1,0:T(8,128)S(1)} %stack.85, ...), channel_id=1, replica_groups=mesh['dp'=8,'tensor'=4] {'dp'}, use_global_device_ids=true, to_apply=%region_28.29 | all-reduce | flops 20736 | bytes 156672 | tf_op jit(solution)/shard_map/psum | solution.py:381
  514.3 51.2 %reduce-scatter.32.cloned.1.call-done = f32[96,768]{1,0:T(8,128)} async-done(((f32[768,768]{1,0:T(8,128)}), f32[96,768]{1,0:T(8,128)}) %reduce-scatter.32.cloned.1.call-update) | async-done | bytes 294928 | tf_op jit(solution)/shard_map/reduce_scatter | solution.py:378
  565.5 65.3 %reduce-scatter.28.cloned.1.call-done = f32[96,192]{1,0:T(8,128)} async-done(((f32[768,192]{1,0:T(8,128)}), f32[96,192]{1,0:T(8,128)}) %reduce-scatter.28.cloned.1.call-update) | async-done | bytes 73744 | tf_op jit(solution)/shard_map/reduce_scatter | solution.py:376
  630.8 72.3 %reduce-scatter.26.cloned.1.call-done = f32[96,3,192]{2,0,1:T(8,128)} async-done(((f32[768,3,192]{2,0,1:T(8,128)}), f32[96,3,192]{2,0,1:T(8,128)}) %reduce-scatter.26.cloned.1.call-update) | async-done | bytes 221200 | tf_op jit(solution)/shard_map/reduce_scatter | solution.py:375
  703.1 131.2 %all-reduce.10.cloned.1.call-done = f32[1001,768]{1,0:T(8,128)} async-done(((f32[1001,768]{1,0:T(8,128)}), f32[1001,768]{1,0:T(8,128)}) %all-reduce.10.cloned.1.call-update) | async-done | bytes 3075088 | tf_op jit(solution)/shard_map/psum | solution.py:381
  834.2 233.0 %reduce-scatter.24.cloned.1.call-done = f32[576,768]{1,0:T(8,128)} async-done(((f32[4608,768]{1,0:T(8,128)}), f32[576,768]{1,0:T(8,128)}) %reduce-scatter.24.cloned.1.call-update) | async-done | bytes 1769488 | tf_op jit(solution)/shard_map/reduce_scatter | solution.py:379
  (415 shorter events, 143.5 us)
Async XLA Ops:
  7.2 62.8 %reduce-scatter.12.cloned.1.call-start = ((), (), s32[]{:S(2)}) async-start(), calls=%async_computation.11 | async-start | bytes 1966080 | tf_op jit(solution)/shard_map/reduce_scatter | solution.py:221
  19.2 54.6 %copy-start.34 = (f32[768]{0:T(1024)}, f32[768]{0:T(1024)S(1)}, u32[]{:S(2)}) copy-start(f32[768]{0:T(1024)S(1)} %get-tuple-element.56) | copy-start | bytes 9220
  19.2 54.6 %copy-start.86 = (f32[768]{0:T(1024)}, f32[768]{0:T(1024)S(1)}, u32[]{:S(2)}) copy-start(f32[768]{0:T(1024)S(1)} %get-tuple-element.55) | copy-start | bytes 9220
  19.2 116.7 %copy-start.29 = (f32[768]{0:T(1024)}, f32[768]{0:T(1024)S(1)}, u32[]{:S(2)}) copy-start(f32[768]{0:T(1024)S(1)} %get-tuple-element.59) | copy-start | bytes 9220
  19.5 122.3 %copy-start.56 = (f32[768]{0:T(1024)}, f32[768]{0:T(1024)S(1)}, u32[]{:S(2)}) copy-start(f32[768]{0:T(1024)S(1)} %get-tuple-element.45) | copy-start | bytes 9220
  39.0 57.0 %all-gather.6.cloned.1.call-start = ((), (), s32[]{:S(2)}) async-start(), calls=%async_computation.12 | async-start | bytes 1966080 | tf_op jit(solution)/shard_map/all_gather | solution.py:233
  39.4 96.5 %copy-start.26 = (f32[768]{0:T(1024)}, f32[768]{0:T(1024)S(1)}, u32[]{:S(2)}) copy-start(f32[768]{0:T(1024)S(1)} %convert_element_type.211) | copy-start | bytes 9220
  39.4 96.5 %copy-start.31 = (f32[256]{0:T(256)}, f32[256]{0:T(256)S(1)}, u32[]{:S(2)}) copy-start(f32[256]{0:T(256)S(1)} %fusion.141) | copy-start | bytes 3076
  42.9 96.5 %copy-start.2 = (f32[1,1024,768]{2,1,0:T(8,128)}, f32[1,1024,768]{2,1,0:T(8,128)S(1)}, u32[]{:S(2)}) copy-start(f32[1,1024,768]{2,1,0:T(8,128)S(1)} %get-tuple-element.15) | copy-start | bytes 9437188
  76.2 59.7 %reduce-scatter.14.cloned.1.call-start = ((), (), s32[]{:S(2)}) async-start(), calls=%async_computation.13 | async-start | bytes 1966080 | tf_op jit(solution)/shard_map/reduce_scatter | solution.py:241
  107.6 88.1 %reduce-scatter.16.cloned.1.call-start = ((), (), s32[]{:S(2)}) async-start(), calls=%async_computation.15 | async-start | bytes 1966080 | tf_op jit(solution)/shard_map/reduce_scatter | solution.py:221
  161.4 34.3 %copy-start.32 = (f32[256]{0:T(256)S(1)}, f32[256]{0:T(256)}, u32[]{:S(2)}) copy-start(f32[256]{0:T(256)} %copy-done.31) | copy-start | bytes 3076
  167.4 51.6 %copy-start.110 = (f32[768]{0:T(1024)S(1)}, f32[768]{0:T(1024)}, u32[]{:S(2)}) copy-start(f32[768]{0:T(1024)} %copy-done.109) | copy-start | bytes 9220
  167.4 51.6 %all-gather.10.cloned.1.call-start = ((), (), s32[]{:S(2)}) async-start(), calls=%async_computation.16 | async-start | bytes 1966080 | tf_op jit(solution)/shard_map/all_gather | solution.py:233
  197.3 92.0 %copy-start.82 = (f32[256]{0:T(256)}, f32[256]{0:T(256)S(1)}, u32[]{:S(2)}) copy-start(f32[256]{0:T(256)S(1)} %broadcast_multiply_fusion.5) | copy-start | bytes 3076
  198.1 91.1 %copy-start.102 = (f32[256]{0:T(256)}, f32[256]{0:T(256)S(1)}, u32[]{:S(2)}) copy-start(f32[256]{0:T(256)S(1)} %fusion.135) | copy-start | bytes 3076
  199.2 41.0 %all-gather.8.cloned.1.call-start = ((), (), s32[]{:S(2)}) async-start(), calls=%async_computation.14 | async-start | bytes 1966080 | tf_op jit(solution)/shard_map/all_gather | solution.py:291
  199.9 87.7 %reduce-scatter.18.cloned.1.call-start = ((), (), s32[]{:S(2)}) async-start(), calls=%async_computation.17 | async-start | bytes 1966080 | tf_op jit(solution)/shard_map/reduce_scatter | solution.py:305
  259.3 54.4 %all-gather.12.cloned.1.call-start = ((), (), s32[]{:S(2)}) async-start(), calls=%async_computation.18 | async-start | bytes 1966080 | tf_op jit(solution)/shard_map/all_gather | solution.py:317
  293.8 73.9 %reduce-scatter.20.cloned.1.call-start = ((), (), s32[]{:S(2)}) async-start(), calls=%async_computation.19 | async-start | bytes 1966080 | tf_op jit(solution)/shard_map/reduce_scatter | solution.py:325
  339.4 49.5 %all-gather.14.cloned.1.call-start = ((), (), s32[]{:S(2)}) async-start(), calls=%async_computation.20 | async-start | bytes 1966080 | tf_op jit(solution)/shard_map/all_gather | solution.py:333
  367.8 52.0 %reduce-scatter.22.cloned.1.call-start = ((), (), s32[]{:S(2)}) async-start(), calls=%async_computation.21 | async-start | bytes 1966080 | tf_op jit(solution)/shard_map/reduce_scatter | solution.py:241
  370.4 143.9 %reduce-scatter.30.cloned.1.call-start = ((), (), s32[]{:S(2)}) async-start(), calls=%async_computation.26 | async-start | bytes 2654208 | tf_op jit(solution)/shard_map/reduce_scatter | solution.py:377
  375.6 189.8 %reduce-scatter.32.cloned.1.call-start = ((), (), s32[]{:S(2)}) async-start(), calls=%async_computation.27 | async-start | bytes 2654208 | tf_op jit(solution)/shard_map/reduce_scatter | solution.py:378
  380.1 250.7 %reduce-scatter.28.cloned.1.call-start = ((), (), s32[]{:S(2)}) async-start(), calls=%async_computation.25 | async-start | bytes 884736 | tf_op jit(solution)/shard_map/reduce_scatter | solution.py:376
  383.1 319.9 %reduce-scatter.26.cloned.1.call-start = ((), (), s32[]{:S(2)}) async-start(), calls=%async_computation.24 | async-start | bytes 2654208 | tf_op jit(solution)/shard_map/reduce_scatter | solution.py:375
  388.0 446.3 %all-reduce.10.cloned.1.call-start = ((), (), s32[]{:S(2)}) async-start(), calls=%async_computation.22 | async-start | bytes 6193152 | tf_op jit(solution)/shard_map/psum | solution.py:381
  439.4 627.9 %reduce-scatter.24.cloned.1.call-start = ((), (), s32[]{:S(2)}) async-start(), calls=%async_computation.23 | async-start | bytes 15925248 | tf_op jit(solution)/shard_map/reduce_scatter | solution.py:379
  463.8 44.7 %copy-start.33 = (f32[256]{0:T(256)S(1)}, f32[256]{0:T(256)}, u32[]{:S(2)}) copy-start(f32[256]{0:T(256)} %copy-done.31) | copy-start | bytes 3076
  463.8 44.7 %copy-start.37 = (f32[768]{0:T(1024)S(1)}, f32[768]{0:T(1024)}, u32[]{:S(2)}) copy-start(f32[768]{0:T(1024)} %copy-done.36) | copy-start | bytes 9220
  468.0 44.0 %copy-start.14 = (f32[256,768]{1,0:T(8,128)S(1)}, f32[256,768]{1,0:T(8,128)}, u32[]{:S(2)}) copy-start(f32[256,768]{1,0:T(8,128)} %copy-done.12) | copy-start | bytes 2359300
  512.0 559.0 %copy-start.1 = (bf16[1001,768]{1,0:T(8,128)(2,1)S(1)}, bf16[1001,768]{1,0:T(8,128)(2,1)}, u32[]{:S(2)}) copy-start(bf16[1001,768]{1,0:T(8,128)(2,1)} %param.22) | copy-start | bytes 4612612
  (105 other events, 1140.9 us)
Sparse Core Ops, SparseCore 0:
  39.1 30.8 reduce-scatter.11
  76.3 19.6 all-gather.5
  107.7 28.1 reduce-scatter.13
  167.5 28.1 reduce-scatter.15
  199.3 19.6 all-gather.9
  220.5 19.6 all-gather.7
  259.4 28.1 reduce-scatter.17
  294.0 19.6 all-gather.11
  339.6 28.1 reduce-scatter.19
  369.2 19.6 all-gather.13
  391.6 28.1 reduce-scatter.21
  423.7 69.4 reduce-scatter.29
  497.3 68.1 reduce-scatter.31
  569.2 61.5 reduce-scatter.27
  635.1 67.8 reduce-scatter.25
  707.6 126.5 all-reduce.9
  838.8 228.4 reduce-scatter.23
where the time goes:
time: 1090 us; the launch traced here: 1080 us
  waiting for transfers between devices  779 us (71%)
  other arithmetic  99.6 us (9%)
  matrix products  75 us (7%)
  blocking collectives  52.1 us (5%)
  local copies, waits for them, and re-layouts  51.1 us (5%)
  between operations  18.2 us (2%)
    reduce_scatter x1, waiting for transfers between devices, shards(): lax.psum_scatter(grad_w_mod, 'dp', scatter_dimension=0, tiled=True)  233 us
    psum x1, waiting for transfers between devices, shards(): lax.psum((grad_k_att, grad_k_ffn, grad_b_up, grad_b_out, grad_b_down, gra...  131 us
    reduce_scatter x1, waiting for transfers between devices, shards(): lax.psum_scatter(grad_w_qkv, 'dp', scatter_dimension=0, tiled=True)  72.3 us
    reduce_scatter x1, waiting for transfers between devices, shards(): lax.psum_scatter(grad_w_out, 'dp', scatter_dimension=0, tiled=True)  65.3 us
    reduce_scatter x2, waiting for transfers between devices, forward_pass(): lax.psum_scatter(contract_last(attended, w_out).astype(jnp.bfloat16), 'te...  55.4 us
    reduce_scatter x1, waiting for transfers between devices, shards(): lax.psum_scatter(grad_w_down, 'dp', scatter_dimension=0, tiled=True)  51.2 us
    reduce_scatter x2, waiting for transfers between devices, forward_pass(): lax.psum_scatter(contract_last(activated, w_down).astype(jnp.bfloat16), '...  44.2 us
    psum x1, blocking collectives, shards(): lax.psum((grad_k_att, grad_k_ffn, grad_b_up, grad_b_out, grad_b_down, gra...  40.3 us
  transfers between devices with their start and end apart: 17, of which 16 were waited for; matrix products, arithmetic and copies ran while one was open for 8% of the time, Pallas kernels for 0%

commit v1 on v0

--- a/solution.py
+++ b/solution.py
@@ -9,6 +9,22 @@
 norm_eps = 1e-06
 score_scale = 0.125
 highest = lax.Precision.HIGHEST
+
+
+def perform_plane(xx, axis_key):
+    q_next, finding, local_next = (lax.axis_size(axis_key), lax.axis_index(axis_key), xx.shape[0])
+    chunks = tuple((idx * q_next if jj == 0 else idx for jj, idx in enumerate(xx.shape)))
+    reached = lax.dynamic_update_slice_in_dim(
+        jnp.zeros(chunks, xx.dtype), xx, finding * local_next, axis=0
+    )
+    for t in range(1, q_next):
+        xx = lax.ppermute(
+            xx, axis_name=axis_key, perm=tuple(((jj, (jj + 1) % q_next) for jj in range(q_next)))
+        )
+        reached = lax.dynamic_update_slice_in_dim(
+            reached, xx, (finding - t) % q_next * local_next, axis=0
+        )
+    return reached
 
 
 def layer_norm(values):
@@ -230,7 +246,7 @@
         middle = source_share + gate_att_rows * branch
         normed_ffn = layer_norm(middle)
         shaped_share = (normed_ffn * (1.0 + scale_ffn_rows) + shift_ffn_rows).astype(jnp.bfloat16)
-        shaped_ffn = lax.all_gather(shaped_share, "tensor", axis=0, tiled=True)
+        shaped_ffn = perform_plane(shaped_share, "tensor")
         hidden = jnp.dot(shaped_ffn, w_up, preferred_element_type=jnp.float32) + b_up.astype(
             jnp.float32
         )

time: 1090 us -> 1100 us (level)
  local copies, waits for them, and re-layouts: 51.1 us -> 64.1 us
    ppermute x0 -> x6, waiting for transfers between devices: none -> 42.3 us  [perform_plane(): lax.ppermute(xx, axis_name=axis_key, perm=tuple(((jj, (jj + 1) % q_next)...]
    all_gather x2 -> x0, waiting for transfers between devices: 38.4 us -> none  [forward_pass(): shaped_ffn = lax.all_gather(shaped_share, 'tensor', axis=0, tiled=True)]
  transfers between devices with their start and end apart: 17 -> 21, of which waited for: 16 -> 19; matrix products, arithmetic and copies ran while one was open for 8% -> 9% of each run, Pallas kernels for 0% -> 0%
where the time goes in v1:
time: 1100 us; the launch traced here: 1090 us
  waiting for transfers between devices  774 us (70%)
  other arithmetic  100 us (9%)
  matrix products  75 us (7%)
  local copies, waits for them, and re-layouts  64.1 us (6%)
  blocking collectives  52.1 us (5%)
  between operations  18.2 us (2%)
    reduce_scatter x1, waiting for transfers between devices, shards(): lax.psum_scatter(grad_w_mod, 'dp', scatter_dimension=0, tiled=True)  233 us
    psum x1, waiting for transfers between devices, shards(): lax.psum((grad_k_att, grad_k_ffn, grad_b_up, grad_b_out, grad_b_down, gra...  131 us
    reduce_scatter x1, waiting for transfers between devices, shards(): lax.psum_scatter(grad_w_qkv, 'dp', scatter_dimension=0, tiled=True)  72.4 us
    reduce_scatter x1, waiting for transfers between devices, shards(): lax.psum_scatter(grad_w_out, 'dp', scatter_dimension=0, tiled=True)  65.2 us
    reduce_scatter x2, waiting for transfers between devices, forward_pass(): lax.psum_scatter(contract_last(attended, w_out).astype(jnp.bfloat16), 'te...  55.4 us
    reduce_scatter x1, waiting for transfers between devices, shards(): lax.psum_scatter(grad_w_down, 'dp', scatter_dimension=0, tiled=True)  51.2 us
    reduce_scatter x2, waiting for transfers between devices, forward_pass(): lax.psum_scatter(contract_last(activated, w_down).astype(jnp.bfloat16), '...  46.1 us
    ppermute x6, waiting for transfers between devices, perform_plane(): lax.ppermute(xx, axis_name=axis_key, perm=tuple(((jj, (jj + 1) % q_next)...  42.3 us
  transfers between devices with their start and end apart: 21, of which 19 were waited for; matrix products, arithmetic and copies ran while one was open for 9% of the time, Pallas kernels for 0%

profile of v1, /device:TPU:0, one launch (start us, length us, event | category | flops | bytes accessed | tf_op | source)
XLA Modules:
  0.0 1086.3 jit_solution(9851774591386597575)
XLA Ops:
  13.5 5.1 convolution_reduce_fusion
  20.1 4.5 fusion.23
  27.6 5.4 reshape_reshape.15
  42.9 27.1 %reduce-scatter.12.cloned.1.call-done = bf16[256,768]{1,0:T(8,128)(2,1)} async-done(((bf16[1024,768]{1,0:T(8,128)(2,1)}), bf16[256,768]{1,0:T(8,128)(2,1)}) %reduce-scatter.12.cloned.1.call-update) | async-done | bytes 393232 | tf_op jit(solution)/shard_map/reduce_scatter | solution.py:237
  77.4 7.2 collective-permute-done
  85.3 7.3 collective-permute-done.1
  105.2 4.4 fusion.39
  115.3 27.2 %reduce-scatter.14.cloned.1.call-done = bf16[256,768]{1,0:T(8,128)(2,1)} async-done(((bf16[1024,768]{1,0:T(8,128)(2,1)}), bf16[256,768]{1,0:T(8,128)(2,1)}) %reduce-scatter.14.cloned.1.call-update) | async-done | bytes 393232 | tf_op jit(solution)/shard_map/reduce_scatter | solution.py:257
  148.5 4.5 add_convert_fusion
  155.9 5.4 reshape_reshape.16
  174.1 28.3 %reduce-scatter.16.cloned.1.call-done = bf16[256,768]{1,0:T(8,128)(2,1)} async-done(((bf16[1024,768]{1,0:T(8,128)(2,1)}), bf16[256,768]{1,0:T(8,128)(2,1)}) %reduce-scatter.16.cloned.1.call-update) | async-done | bytes 393232 | tf_op jit(solution)/shard_map/reduce_scatter | solution.py:237
  207.0 7.4 collective-permute-done.3
  214.5 15.2 %collective-permute-done.4 = bf16[256,768]{1,0:T(8,128)(2,1)S(1)} collective-permute-done((bf16[256,768]{1,0:T(8,128)(2,1)}, bf16[256,768]{1,0:T(8,128)(2,1)S(1)}, u32[]{:S(2)}, u32[]{:S(2)}) %collective-permute-start.4) | collective-permute-done | bytes 393248 | tf_op jit(solution)/shard_map/ppermute | solution.py:21
  232.4 4.6 collective-permute-done.5
  242.8 5.7 multiply_add_fusion
  248.4 8.5 multiply_reduce_fusion.4
  258.7 5.1 convert_reduce_fusion.1
  267.6 28.2 %reduce-scatter.18.cloned.1.call-done = bf16[256,768]{1,0:T(8,128)(2,1)} async-done(((bf16[1024,768]{1,0:T(8,128)(2,1)}), bf16[256,768]{1,0:T(8,128)(2,1)}) %reduce-scatter.18.cloned.1.call-update) | async-done | bytes 393232 | tf_op jit(solution)/shard_map/reduce_scatter | solution.py:321
  302.3 19.6 %all-gather.6.cloned.1.call-done = bf16[1024,768]{1,0:T(8,128)(2,1)} async-done(((bf16[256,768]{1,0:T(8,128)(2,1)}), bf16[1024,768]{1,0:T(8,128)(2,1)}) %all-gather.6.cloned.1.call-update) | async-done | bytes 1572880 | tf_op jit(solution)/shard_map/all_gather | solution.py:333
  347.7 28.3 %reduce-scatter.20.cloned.1.call-done = bf16[256,768]{1,0:T(8,128)(2,1)} async-done(((bf16[1024,768]{1,0:T(8,128)(2,1)}), bf16[256,768]{1,0:T(8,128)(2,1)}) %reduce-scatter.20.cloned.1.call-update) | async-done | bytes 393232 | tf_op jit(solution)/shard_map/reduce_scatter | solution.py:341
  379.2 4.7 fusion.156
  391.5 4.7 fusion.154
  409.3 18.9 %reduce-scatter.22.cloned.1.call-done = bf16[256,768]{1,0:T(8,128)(2,1)} async-done(((bf16[1024,768]{1,0:T(8,128)(2,1)}), bf16[256,768]{1,0:T(8,128)(2,1)}) %reduce-scatter.22.cloned.1.call-update) | async-done | bytes 393232 | tf_op jit(solution)/shard_map/reduce_scatter | solution.py:257
  429.9 11.8 %psum.56 = bf16[1,4608]{1,0:T(2,128)(2,1)S(1)} all-reduce(f32[1,4608]{1,0:T(1,128)S(1)} %convolution_dynamic-update-slice_fusion.1), channel_id=1, replica_groups=mesh['dp'=8,'tensor'=4] {'tensor'}, use_global_device_ids=true, to_apply=%region_25.26 | all-reduce | flops 4608 | bytes 27648 | tf_op jit(solution)/shard_map/psum | solution.py:377
  448.1 6.0 broadcast_multiply_fusion
  455.1 13.3 %multiply_reduce_fusion = (f32[768]{0:T(1024)S(1)}, f32[768]{0:T(1024)S(1)}, f32[768]{0:T(1024)S(1)}, f32[768]{0:T(1024)S(1)}, f32[768]{0:T(1024)S(1)}, /*index=...) fusion(f32[1,32,32,768]{3,2,1,0:T(8,128)} %bitcast.206, f32[1024,768]{1,0:T(8,128)} %copy-done.11), kind=kLoop, calls=%fused_computation.141 | loop fusion | flops 12576768 | bytes 6316032 | tf_op jit(solution)/shard_map/reduce_sum | solution.py:74
  476.6 40.3 %all-reduce.11 = (f32[4608]{0:T(1024)}, f32[9,768]{1,0:T(8,128)}, f32[768]{0:T(1024)}, f32[768]{0:T(1024)}, f32[9,768]{1,0:T(8,128)}, /*index=5*/f32[768]{0:T(1024)}) all-reduce(bf16[4608]{0:T(1024)(128)(2,1)S(1)} %convert_reduce_fusion.4, f32[9,768]{1,0:T(8,128)S(1)} %stack.85, ...), channel_id=1, replica_groups=mesh['dp'=8,'tensor'=4] {'dp'}, use_global_device_ids=true, to_apply=%region_28.29 | all-reduce | flops 20736 | bytes 156672 | tf_op jit(solution)/shard_map/psum | solution.py:397
  522.8 51.2 %reduce-scatter.32.cloned.1.call-done = f32[96,768]{1,0:T(8,128)} async-done(((f32[768,768]{1,0:T(8,128)}), f32[96,768]{1,0:T(8,128)}) %reduce-scatter.32.cloned.1.call-update) | async-done | bytes 294928 | tf_op jit(solution)/shard_map/reduce_scatter | solution.py:394
  574.0 65.2 %reduce-scatter.28.cloned.1.call-done = f32[96,192]{1,0:T(8,128)} async-done(((f32[768,192]{1,0:T(8,128)}), f32[96,192]{1,0:T(8,128)}) %reduce-scatter.28.cloned.1.call-update) | async-done | bytes 73744 | tf_op jit(solution)/shard_map/reduce_scatter | solution.py:392
  639.2 72.4 %reduce-scatter.26.cloned.1.call-done = f32[96,3,192]{2,0,1:T(8,128)} async-done(((f32[768,3,192]{2,0,1:T(8,128)}), f32[96,3,192]{2,0,1:T(8,128)}) %reduce-scatter.26.cloned.1.call-update) | async-done | bytes 221200 | tf_op jit(solution)/shard_map/reduce_scatter | solution.py:391
  711.6 131.2 %all-reduce.10.cloned.1.call-done = f32[1001,768]{1,0:T(8,128)} async-done(((f32[1001,768]{1,0:T(8,128)}), f32[1001,768]{1,0:T(8,128)}) %all-reduce.10.cloned.1.call-update) | async-done | bytes 3075088 | tf_op jit(solution)/shard_map/psum | solution.py:397
  842.9 233.0 %reduce-scatter.24.cloned.1.call-done = f32[576,768]{1,0:T(8,128)} async-done(((f32[4608,768]{1,0:T(8,128)}), f32[576,768]{1,0:T(8,128)}) %reduce-scatter.24.cloned.1.call-update) | async-done | bytes 1769488 | tf_op jit(solution)/shard_map/reduce_scatter | solution.py:395
  (435 shorter events, 166.1 us)
Async XLA Ops:
  7.2 62.8 %reduce-scatter.12.cloned.1.call-start = ((), (), s32[]{:S(2)}) async-start(), calls=%async_computation.11 | async-start | bytes 1966080 | tf_op jit(solution)/shard_map/reduce_scatter | solution.py:237
  19.2 55.8 %copy-start.36 = (f32[768]{0:T(1024)}, f32[768]{0:T(1024)S(1)}, u32[]{:S(2)}) copy-start(f32[768]{0:T(1024)S(1)} %get-tuple-element.56) | copy-start | bytes 9220
  19.2 123.3 %copy-start.31 = (f32[768]{0:T(1024)}, f32[768]{0:T(1024)S(1)}, u32[]{:S(2)}) copy-start(f32[768]{0:T(1024)S(1)} %get-tuple-element.59) | copy-start | bytes 9220
  39.0 103.5 %reduce-scatter.14.cloned.1.call-start = ((), (), s32[]{:S(2)}) async-start(), calls=%async_computation.12 | async-start | bytes 1966080 | tf_op jit(solution)/shard_map/reduce_scatter | solution.py:257
  39.4 103.1 %copy-start.28 = (f32[768]{0:T(1024)}, f32[768]{0:T(1024)S(1)}, u32[]{:S(2)}) copy-start(f32[768]{0:T(1024)S(1)} %convert_element_type.211) | copy-start | bytes 9220
  39.4 103.1 %copy-start.33 = (f32[256]{0:T(256)}, f32[256]{0:T(256)S(1)}, u32[]{:S(2)}) copy-start(f32[256]{0:T(256)S(1)} %fusion.141) | copy-start | bytes 3076
  42.9 103.1 %copy-start.2 = (f32[1,1024,768]{2,1,0:T(8,128)}, f32[1,1024,768]{2,1,0:T(8,128)S(1)}, u32[]{:S(2)}) copy-start(f32[1,1024,768]{2,1,0:T(8,128)S(1)} %get-tuple-element.15) | copy-start | bytes 9437188
  77.4 7.2 collective-permute-start
  85.3 7.3 collective-permute-start.1
  92.6 7.5 collective-permute-start.2
  113.5 88.9 %reduce-scatter.16.cloned.1.call-start = ((), (), s32[]{:S(2)}) async-start(), calls=%async_computation.14 | async-start | bytes 1966080 | tf_op jit(solution)/shard_map/reduce_scatter | solution.py:237
  174.0 74.4 %all-gather.4.cloned.1.call-start = ((), (), s32[]{:S(2)}) async-start(), calls=%async_computation.13 | async-start | bytes 1966080 | tf_op jit(solution)/shard_map/all_gather | solution.py:307
  203.9 93.5 %copy-start.85 = (f32[256]{0:T(256)}, f32[256]{0:T(256)S(1)}, u32[]{:S(2)}) copy-start(f32[256]{0:T(256)S(1)} %broadcast_multiply_fusion.5) | copy-start | bytes 3076
  204.2 93.3 %copy-start.103 = (f32[256]{0:T(256)}, f32[256]{0:T(256)S(1)}, u32[]{:S(2)}) copy-start(f32[256]{0:T(256)S(1)} %fusion.135) | copy-start | bytes 3076
  207.0 7.5 collective-permute-start.3
  207.0 88.8 %reduce-scatter.18.cloned.1.call-start = ((), (), s32[]{:S(2)}) async-start(), calls=%async_computation.15 | async-start | bytes 1966080 | tf_op jit(solution)/shard_map/reduce_scatter | solution.py:321
  214.5 15.2 %collective-permute-start.4 = (bf16[256,768]{1,0:T(8,128)(2,1)}, bf16[256,768]{1,0:T(8,128)(2,1)S(1)}, u32[]{:S(2)}, u32[]{:S(2)}) collective-permute-start(bf16[256,768]{1,0:T(8,128)(2,1)} %collective-permute-done.3), channel_id=1, source_target_pairs={{0,1},{1,2},{2,3},{3,0},{4,5},{5,6},{6,7},{7,4},{8,9},{9,10},{10,1... | collective-permute-start | bytes 1179656 | tf_op jit(solution)/shard_map/ppermute | solution.py:21
  229.7 7.4 collective-permute-start.5
  267.5 54.4 %all-gather.6.cloned.1.call-start = ((), (), s32[]{:S(2)}) async-start(), calls=%async_computation.16 | async-start | bytes 1966080 | tf_op jit(solution)/shard_map/all_gather | solution.py:333
  302.1 74.0 %reduce-scatter.20.cloned.1.call-start = ((), (), s32[]{:S(2)}) async-start(), calls=%async_computation.17 | async-start | bytes 1966080 | tf_op jit(solution)/shard_map/reduce_scatter | solution.py:341
  347.7 49.7 %all-gather.8.cloned.1.call-start = ((), (), s32[]{:S(2)}) async-start(), calls=%async_computation.18 | async-start | bytes 1966080 | tf_op jit(solution)/shard_map/all_gather | solution.py:349
  376.1 52.2 %reduce-scatter.22.cloned.1.call-start = ((), (), s32[]{:S(2)}) async-start(), calls=%async_computation.19 | async-start | bytes 1966080 | tf_op jit(solution)/shard_map/reduce_scatter | solution.py:257
  378.7 144.1 %reduce-scatter.30.cloned.1.call-start = ((), (), s32[]{:S(2)}) async-start(), calls=%async_computation.24 | async-start | bytes 2654208 | tf_op jit(solution)/shard_map/reduce_scatter | solution.py:393
  384.0 190.0 %reduce-scatter.32.cloned.1.call-start = ((), (), s32[]{:S(2)}) async-start(), calls=%async_computation.25 | async-start | bytes 2654208 | tf_op jit(solution)/shard_map/reduce_scatter | solution.py:394
  388.5 250.7 %reduce-scatter.28.cloned.1.call-start = ((), (), s32[]{:S(2)}) async-start(), calls=%async_computation.23 | async-start | bytes 884736 | tf_op jit(solution)/shard_map/reduce_scatter | solution.py:392
  391.4 320.2 %reduce-scatter.26.cloned.1.call-start = ((), (), s32[]{:S(2)}) async-start(), calls=%async_computation.22 | async-start | bytes 2654208 | tf_op jit(solution)/shard_map/reduce_scatter | solution.py:391
  396.3 446.6 %all-reduce.10.cloned.1.call-start = ((), (), s32[]{:S(2)}) async-start(), calls=%async_computation.20 | async-start | bytes 6193152 | tf_op jit(solution)/shard_map/psum | solution.py:397
  447.8 628.1 %reduce-scatter.24.cloned.1.call-start = ((), (), s32[]{:S(2)}) async-start(), calls=%async_computation.21 | async-start | bytes 15925248 | tf_op jit(solution)/shard_map/reduce_scatter | solution.py:395
  472.2 44.8 %copy-start.35 = (f32[256]{0:T(256)S(1)}, f32[256]{0:T(256)}, u32[]{:S(2)}) copy-start(f32[256]{0:T(256)} %copy-done.33) | copy-start | bytes 3076
  472.2 44.8 %copy-start.39 = (f32[768]{0:T(1024)S(1)}, f32[768]{0:T(1024)}, u32[]{:S(2)}) copy-start(f32[768]{0:T(1024)} %copy-done.38) | copy-start | bytes 9220
  476.4 44.1 %copy-start.14 = (f32[256,768]{1,0:T(8,128)S(1)}, f32[256,768]{1,0:T(8,128)}, u32[]{:S(2)}) copy-start(f32[256,768]{1,0:T(8,128)} %copy-done.12) | copy-start | bytes 2359300
  520.6 559.1 %copy-start.1 = (bf16[1001,768]{1,0:T(8,128)(2,1)S(1)}, bf16[1001,768]{1,0:T(8,128)(2,1)}, u32[]{:S(2)}) copy-start(bf16[1001,768]{1,0:T(8,128)(2,1)} %param.22) | copy-start | bytes 4612612
  (112 other events, 835.2 us)
Sparse Core Ops, SparseCore 0:
  39.1 30.8 reduce-scatter.11
  113.6 28.8 reduce-scatter.13
  174.1 28.1 reduce-scatter.15
  207.1 24.6 all-gather.3
  267.7 28.1 reduce-scatter.17
  302.2 19.6 all-gather.5
  347.8 28.1 reduce-scatter.19
  377.7 19.6 all-gather.7
  400.1 28.1 reduce-scatter.21
  432.2 69.4 reduce-scatter.29
  505.8 68.1 reduce-scatter.31
  577.7 61.4 reduce-scatter.27
  643.6 67.9 reduce-scatter.25
  716.2 126.6 all-reduce.9
  847.4 228.4 reduce-scatter.23
